TPU v7x, 128 devices: a whole 4x4x4 slice. The times are simulated.
128 devices in a mesh: wide: 32 (over y_lo, x, z), narrow: 4 (over y_hi, core).
Axes of the slice: x: 4, y: 4 (y_hi: 2, y_lo: 2; y = y_hi * 2 + y_lo), z: 4, core: 2. Of those that a mesh axis runs over, the one named last changes fastest.
Arguments:
- trial_x: float32 [262144, 128], P(('wide', 'narrow')), may hold values from -6 to 6
- trial_y: float32 [262144, 128], P(('wide', 'narrow')), may hold values from -6 to 6
- energy: float32 [262144], P(('wide', 'narrow')), may hold values from 1 to 4
- level_shift: float32 [128], replicated, may hold values from 0.1 to 0.5
- resonant_kernel: bfloat16 [1024, 8, 256, 256], P(('wide', 'narrow')), may hold values from -0.0625 to 0.0625
- resonant_list: int32 [1024, 8], P(('wide', 'narrow')), may hold values from 0 to 31, all different within a row
- coupling_kernel: bfloat16 [1024, 8, 256, 256], P(('wide', 'narrow')), may hold values from -0.0625 to 0.0625
- coupling_list: int32 [1024, 8], P(('wide', 'narrow')), may hold values from 0 to 31, all different within a row
- partner: int32 [32, 8192], P('wide'), may hold values from 0 to 8191, each once within a row
- exchange_basis: bfloat16 [262144, 1024], P(('wide', 'narrow')), may hold values from -0.0234375 to 0.0234375
Outputs:
- new_x: float32 [262144, 128], P(('wide', 'narrow'))
- new_y: float32 [262144, 128], P(('wide', 'narrow'))
Inputs may be any that keep to these rules, and one draw needn't show every extreme that they name: `resonant_list`: each row lists 8 different column blocks. `coupling_list`: each row lists 8 different column blocks. `partner`: each row is a permutation of the patch rows.
All inputs are finite; a program needn't handle non-finite values.
Results may differ from a plain program's by a relative error of at most 0.0038.
Values may be sent and summed in bfloat16 or wider, within the bound.
No kernel may reach another device: no remote copies, remote signals or barrier semaphores. Data moves between devices by JAX's collectives and lax.ppermute only.
A program may use at most 128 MiB of HBM per device.

v0:
```python
import jax
import jax.numpy as jnp
from jax import lax
from jax.sharding import PartitionSpec as P

BLK = 256
APPS = 2


def swapped(array, axis, stride):
    return lax.ppermute(array, axis, [(i, i ^ 1 << stride) for i in range(lax.axis_size(axis))])


def block_product(kernel, source, indices):
    columns = source.shape[1]
    tiles = source[indices]
    result = jnp.einsum("bnij,bnjc->bic", kernel, tiles, preferred_element_type=jnp.float32)
    return result.reshape(-1, columns)


def mirror_rows(stacked):
    top_bit = lax.axis_size("wide").bit_length() - 2
    moved = swapped(stacked, "wide", top_bit)
    return lax.all_gather(moved, "narrow", axis=0, tiled=True)


def exchange_term(summed, exchange_basis):
    partial_sum = lax.dot_general(
        exchange_basis, summed, (((0,), (0,)), ((), ())), preferred_element_type=jnp.float32
    )
    weights = lax.psum(partial_sum, ("wide", "narrow"))
    return jnp.dot(exchange_basis, weights.astype(jnp.bfloat16), preferred_element_type=jnp.float32)


def apply_once(
    trial_x,
    trial_y,
    energy,
    level_shift,
    resonant_kernel,
    resonant_list,
    coupling_kernel,
    coupling_list,
    partner,
    exchange_basis,
):
    vectors = trial_x.shape[1]
    stacked = jnp.concatenate([trial_x.astype(jnp.bfloat16), trial_y.astype(jnp.bfloat16)], axis=1)
    own_patch = lax.all_gather(stacked, "narrow", axis=0, tiled=True)
    mirror_patch = mirror_rows(stacked)
    offsets = jnp.arange(BLK, dtype=jnp.int32)
    own_indices = resonant_list[:, :, None] * BLK + offsets
    resonant = block_product(resonant_kernel, own_patch, own_indices)
    partner_indices = partner[0].reshape(-1, BLK)[coupling_list]
    coupling = block_product(coupling_kernel, mirror_patch, partner_indices)
    summed = (trial_x + trial_y).astype(jnp.bfloat16)
    exchange = exchange_term(summed, exchange_basis)
    levels = energy[:, None]
    shifts = level_shift[None, :]
    image_x = levels * trial_x + resonant[:, :vectors] + coupling[:, vectors:] + exchange
    image_y = -(levels * trial_y + resonant[:, vectors:] + coupling[:, :vectors] + exchange)
    next_x = (image_x - shifts * trial_x) / (levels - shifts)
    next_y = -(image_y - shifts * trial_y) / (levels + shifts)
    return (next_x, next_y)


def on_device(
    trial_x,
    trial_y,
    energy,
    level_shift,
    resonant_kernel,
    resonant_list,
    coupling_kernel,
    coupling_list,
    partner,
    exchange_basis,
):
    current_x, current_y = (trial_x, trial_y)
    for app_index in range(APPS):
        current_x, current_y = apply_once(
            current_x,
            current_y,
            energy,
            level_shift,
            resonant_kernel,
            resonant_list,
            coupling_kernel,
            coupling_list,
            partner,
            exchange_basis,
        )
    return (current_x, current_y)


def solution(mesh):
    return jax.shard_map(
        on_device,
        mesh=mesh,
        in_specs=(
            P(("wide", "narrow"), None),
            P(("wide", "narrow"), None),
            P(("wide", "narrow")),
            P(),
            P(("wide", "narrow"), None, None, None),
            P(("wide", "narrow"), None),
            P(("wide", "narrow"), None, None, None),
            P(("wide", "narrow"), None),
            P("wide", None),
            P(("wide", "narrow"), None),
        ),
        out_specs=(P(("wide", "narrow"), None), P(("wide", "narrow"), None)),
        check_vma=False,
    )
```

profile of v0, /device:TPU:1, one launch (start us, length us, event | category | flops | bytes accessed | tf_op | source)
XLA Modules:
  0.0 613.9 jit_solution(15115098581168945599)
XLA Ops:
  7.2 0.0 copy-start.1
  7.2 0.0 copy-start
  7.2 0.0 copy-start.5
  7.2 0.0 copy-start.6
  7.2 0.0 all-gather.5.cloned.1.call-start
  7.3 1.4 convert_element_type.24
  8.7 1.3 convert_element_type.25
  10.0 1.1 pad_maximum_fusion
  11.0 0.0 all-gather.5.cloned.1.call-update
  11.1 0.0 all-gather.7.cloned.1.call-start
  11.1 2.2 collective-permute-start
  13.3 32.0 %collective-permute-done = bf16[2048,256]{1,0:T(8,128)(2,1)S(1)} collective-permute-done((bf16[2048,256]{1,0:T(8,128)(2,1)}, bf16[2048,256]{1,0:T(8,128)(2,1)S(1)}, u32[]{:S(2)}, u32[]{:S(2)}) %collective-permute-start) | collective-permute-done | bytes 1048608 | tf_op jit(solution)/shard_map/ppermute | solution.py:11
  45.3 1.0 copy-done.3
  46.2 0.0 all-gather.7.cloned.1.call-update
  46.3 0.0 all-gather.9.cloned.1.call-start
  46.3 2.6 copy.12
  48.9 1.3 copy.16
  50.2 0.5 broadcast.86
  50.7 0.0 copy-done.5
  50.7 0.7 reduce.3
  51.5 0.1 reshape.62
  51.6 0.7 gather_fusion.1
  52.3 0.1 fusion.2
  52.4 2.9 convolution_bitcast_fusion.3
  55.4 96.2 %all-reduce.2 = bf16[1024,128]{0,1:T(8,128)(2,1)S(1)} all-reduce(f32[1024,128]{0,1:T(8,128)S(1)} %convolution_bitcast_fusion.3), channel_id=1, replica_groups=mesh['wide'=32,'narrow'=4] {'wide','narrow'}, use_global_device_ids=true, to_apply=%region_0.0 | all-reduce | flops 131072 | bytes 786432 | tf_op jit(solution)/shard_map/psum | solution.py:31
  151.6 0.0 all-gather.5.cloned.1.call-done
  151.6 63.6 %gather_fusion = bf16[16384,256]{1,0:T(8,128)(2,1)} fusion(bf16[8192,256]{1,0:T(8,128)(2,1)} %all-gather.5.cloned.1.call-done, s32[16384]{0:T(1024)S(1)} %broadcast_clamp_fusion.1), kind=kCustom, calls=%fused_computation | custom fusion | bytes 16842752 | tf_op jit(solution)/shard_map/gather | solution.py:16
  215.2 8.1 %fusion.10 = f32[8,256,256,1]{1,2,3,0:T(8,128)S(1)} fusion(bf16[8,8,256,256]{3,2,1,0:T(8,128)(2,1)} %param.14, bf16[8,8,256,256]{3,2,1,0:T(8,128)(2,1)} %bitcast.62), kind=kOutput, calls=%fused_computation.34 | convolution fusion | flops 2147483648 | bytes 18874368 | tf_op jit(solution)/shard_map/bnij,bnjc->bic/dot_general | solution.py:17
  223.3 0.1 fusion.8
  223.5 1.4 copy.32
  224.8 1.3 copy.34
  226.1 63.6 %gather_fusion.2 = bf16[16384,256]{1,0:T(8,128)(2,1)} fusion(bf16[8192,256]{1,0:T(8,128)(2,1)} %all-gather.7.cloned.1.call-done, s32[16384]{0:T(1024)S(1)} %broadcast_clamp_fusion), kind=kCustom, calls=%fused_computation.2 | custom fusion | bytes 16842752 | tf_op jit(solution)/shard_map/gather | solution.py:16
  289.8 8.1 %fusion.11 = f32[8,256,256,1]{1,2,3,0:T(8,128)S(1)} fusion(bf16[8,8,256,256]{3,2,1,0:T(8,128)(2,1)} %param.16, bf16[8,8,256,256]{3,2,1,0:T(8,128)(2,1)} %bitcast.63), kind=kOutput, calls=%fused_computation.35 | convolution fusion | flops 2147483648 | bytes 18874368 | tf_op jit(solution)/shard_map/bnij,bnjc->bic/dot_general | solution.py:17
  297.9 0.0 copy-start.8
  297.9 0.0 copy-start.9
  297.9 0.1 fusion.9
  298.0 1.3 copy.33
  299.4 0.3 copy.35
  299.7 6.6 %fusion.5 = (bf16[2048,128]{0,1:T(8,128)(2,1)S(1)}, f32[2048,128]{0,1:T(8,128)}, bf16[2048,128]{0,1:T(8,128)(2,1)S(1)}, f32[2048,128]{0,1:T(8,128)}) fusion(f32[2048,128]{0,1:T(8,128)} %copy.16, f32[128]{0:T(128)S(1)} %copy-done.9, f32[2048,128]{0,1:T(8,128)S(1)} %copy.35, f32[2048,128]{0,1:T(8,128)} %copy.34, f32[2048]{0:T(1024)S(1)} %copy-done.8, ...), kind=kOutput, calls=%fused_computation.29 | convolution fusion | flops 542113792 | bytes 13902336 | tf_op jit(solution)/shard_map/dot_general | solution.py:32
  306.4 1.0 pad_maximum_fusion.1
  307.4 0.0 all-gather.9.cloned.1.call-update
  307.4 0.0 all-gather.11.cloned.1.call-start
  307.5 0.3 collective-permute-start.1
  307.7 40.2 %collective-permute-done.1 = bf16[2048,256]{0,1:T(8,128)(2,1)S(1)} collective-permute-done((bf16[2048,256]{0,1:T(8,128)(2,1)}, bf16[2048,256]{0,1:T(8,128)(2,1)S(1)}, u32[]{:S(2)}, u32[]{:S(2)}) %collective-permute-start.1) | collective-permute-done | bytes 1048608 | tf_op jit(solution)/shard_map/ppermute | solution.py:11
  348.0 1.0 copy-done.4
  348.9 0.0 all-gather.11.cloned.1.call-update
  349.0 3.5 convolution_bitcast_fusion.2
  352.5 84.9 %all-reduce.3 = bf16[1024,128]{0,1:T(8,128)(2,1)S(1)} all-reduce(f32[1024,128]{0,1:T(8,128)S(1)} %convolution_bitcast_fusion.2), channel_id=1, replica_groups=mesh['wide'=32,'narrow'=4] {'wide','narrow'}, use_global_device_ids=true, to_apply=%region_1.0 | all-reduce | flops 131072 | bytes 786432 | tf_op jit(solution)/shard_map/psum | solution.py:31
  437.4 0.0 all-gather.9.cloned.1.call-done
  437.5 6.4 %copy.20 = bf16[8192,256]{1,0:T(8,128)(2,1)} copy(bf16[8192,256]{0,1:T(8,128)(2,1)} %all-gather.9.cloned.1.call-done) | data formatting | bytes 8388608 | tf_op jit(solution)/shard_map/all_gather | solution.py:49
  443.9 63.6 %gather_fusion.3 = bf16[16384,256]{1,0:T(8,128)(2,1)} fusion(bf16[8192,256]{1,0:T(8,128)(2,1)} %copy.20, s32[16384]{0:T(1024)S(1)} %broadcast_clamp_fusion.1), kind=kCustom, calls=%fused_computation.3 | custom fusion | bytes 16842752 | tf_op jit(solution)/shard_map/gather | solution.py:16
  507.5 8.1 %fusion.12 = f32[8,256,256,1]{1,2,3,0:T(8,128)S(1)} fusion(bf16[8,8,256,256]{3,2,1,0:T(8,128)(2,1)} %param.14, bf16[8,8,256,256]{3,2,1,0:T(8,128)(2,1)} %bitcast.60), kind=kOutput, calls=%fused_computation.36 | convolution fusion | flops 2147483648 | bytes 18874368 | tf_op jit(solution)/shard_map/bnij,bnjc->bic/dot_general | solution.py:17
  515.6 0.1 fusion.6
  515.7 0.3 copy.36
  516.1 1.3 copy.38
  517.4 6.4 %copy.22 = bf16[8192,256]{1,0:T(8,128)(2,1)} copy(bf16[8192,256]{0,1:T(8,128)(2,1)} %all-gather.11.cloned.1.call-done) | data formatting | bytes 8388608 | tf_op jit(solution)/shard_map/all_gather | solution.py:24
  523.7 63.6 %gather_fusion.4 = bf16[16384,256]{1,0:T(8,128)(2,1)} fusion(bf16[8192,256]{1,0:T(8,128)(2,1)} %copy.22, s32[16384]{0:T(1024)S(1)} %broadcast_clamp_fusion), kind=kCustom, calls=%fused_computation.4 | custom fusion | bytes 16842752 | tf_op jit(solution)/shard_map/gather | solution.py:16
  587.4 8.1 %fusion.13 = f32[8,256,256,1]{1,2,3,0:T(8,128)S(1)} fusion(bf16[8,8,256,256]{3,2,1,0:T(8,128)(2,1)} %param.16, bf16[8,8,256,256]{3,2,1,0:T(8,128)(2,1)} %bitcast.61), kind=kOutput, calls=%fused_computation.37 | convolution fusion | flops 2147483648 | bytes 18874368 | tf_op jit(solution)/shard_map/bnij,bnjc->bic/dot_general | solution.py:17
  595.5 0.1 fusion.7
  595.6 1.3 copy.37
  596.9 0.3 copy.39
  597.3 6.2 %add_divide_fusion = (f32[2048,128]{0,1:T(8,128)S(1)}, f32[2048,128]{0,1:T(8,128)}) fusion(f32[2048,128]{0,1:T(8,128)} %get-tuple-element.7, f32[2048,128]{0,1:T(8,128)S(1)} %copy.39, f32[2048,128]{0,1:T(8,128)} %copy.38, f32[128]{0:T(128)S(1)} %copy-done.9, f32[2048]{0:T(1024)S(1)} %copy-done.8, f32[2048,128]{0,1:T(8,128)} %get-tuple-element.19, ...), kind=kOutput, calls=%fused_computation.7 | convolution fusion | flops 541589504 | bytes 12853760 | tf_op jit(solution)/shard_map/dot_general | solution.py:32
  603.5 2.5 copy.24
  606.0 1.3 copy.25
  (22 shorter events, 0.2 us)
Async XLA Ops:
  7.2 45.3 %copy-start.1 = (f32[2048,128]{1,0:T(8,128)S(1)}, f32[2048,128]{1,0:T(8,128)}, u32[]{:S(2)}) copy-start(f32[2048,128]{1,0:T(8,128)} %param.10) | copy-start | bytes 3145732
  7.2 41.7 %copy-start = (f32[2048,128]{1,0:T(8,128)S(1)}, f32[2048,128]{1,0:T(8,128)}, u32[]{:S(2)}) copy-start(f32[2048,128]{1,0:T(8,128)} %param.11) | copy-start | bytes 3145732
  7.2 43.5 %copy-start.5 = (s32[1,8192]{1,0:T(1,128)S(1)}, s32[1,8192]{1,0:T(1,128)}, u32[]{:S(2)}) copy-start(s32[1,8192]{1,0:T(1,128)} %param.18) | copy-start | bytes 98308
  7.2 44.2 %copy-start.6 = (s32[8,8]{1,0:T(8,128)S(1)}, s32[8,8]{1,0:T(8,128)}, u32[]{:S(2)}) copy-start(s32[8,8]{1,0:T(8,128)} %param.17) | copy-start | bytes 772
  7.2 45.1 %copy-start.7 = (s32[8,8]{1,0:T(8,128)S(1)}, s32[8,8]{1,0:T(8,128)}, u32[]{:S(2)}) copy-start(s32[8,8]{1,0:T(8,128)} %param.15) | copy-start | bytes 772
  7.2 144.4 %all-gather.5.cloned.1.call-start = ((), (), s32[]{:S(2)}) async-start(), calls=%async_computation | async-start | bytes 5242880 | tf_op jit(solution)/shard_map/all_gather | solution.py:49
  11.1 215.1 %all-gather.7.cloned.1.call-start = ((), (), s32[]{:S(2)}) async-start(), calls=%async_computation.1 | async-start | bytes 5242880 | tf_op jit(solution)/shard_map/all_gather | solution.py:24
  11.1 34.2 %collective-permute-start = (bf16[2048,256]{1,0:T(8,128)(2,1)}, bf16[2048,256]{1,0:T(8,128)(2,1)S(1)}, u32[]{:S(2)}, u32[]{:S(2)}) collective-permute-start(bf16[2048,256]{1,0:T(8,128)(2,1)} %pad_maximum_fusion), channel_id=1, source_target_pairs={{0,64},{4,68},{8,72},{12,76},{16,80},{20,84},{24,88},{28,92},{32,9... | collective-permute-start | bytes 3145736 | tf_op jit(solution)/shard_map/ppermute | solution.py:11
  45.3 1.0 copy-start.3
  46.3 391.2 %all-gather.9.cloned.1.call-start = ((), (), s32[]{:S(2)}) async-start(), calls=%async_computation.2 | async-start | bytes 5242880 | tf_op jit(solution)/shard_map/all_gather | solution.py:49
  297.8 1.8 copy-start.2
  297.9 1.8 copy-start.8
  297.9 1.8 copy-start.9
  307.4 209.9 %all-gather.11.cloned.1.call-start = ((), (), s32[]{:S(2)}) async-start(), calls=%async_computation.3 | async-start | bytes 5242880 | tf_op jit(solution)/shard_map/all_gather | solution.py:24
  307.5 40.5 %collective-permute-start.1 = (bf16[2048,256]{0,1:T(8,128)(2,1)}, bf16[2048,256]{0,1:T(8,128)(2,1)S(1)}, u32[]{:S(2)}, u32[]{:S(2)}) collective-permute-start(bf16[2048,256]{0,1:T(8,128)(2,1)} %pad_maximum_fusion.1), channel_id=1, source_target_pairs={{0,64},{4,68},{8,72},{12,76},{16,80},{20,84},{24,88},{28,92},{32,9... | collective-permute-start | bytes 3145736 | tf_op jit(solution)/shard_map/ppermute | solution.py:11
  348.0 1.0 copy-start.4
Sparse Core Ops, SparseCore 0:
  11.2 52.8 all-gather.4
  65.7 38.9 all-gather.6
  307.5 51.1 all-gather.8
  360.3 35.7 all-gather.10
where the time goes:
time: 615 us; the launch traced here: 614 us
  local copies, waits for them, and re-layouts  286 us (47%)
  blocking collectives  181 us (29%)
  waiting for transfers between devices  72.3 us (12%)
  matrix products  51.7 us (8%)
  between operations  14.1 us (2%)
    gather x4, local copies, waits for them, and re-layouts, block_product(): tiles = source[indices]  254 us
    psum x2, blocking collectives, exchange_term(): weights = lax.psum(partial_sum, ('wide', 'narrow'))  181 us
    ppermute x2, waiting for transfers between devices, swapped(): lax.ppermute(array, axis, [(i, i ^ 1 << stride) for i in range(lax.axis_s...  72.2 us
    dot_general x4, matrix products, block_product(): jnp.einsum('bnij,bnjc->bic', kernel, tiles, preferred_element_type=jnp.fl...  32.4 us
    unnamed x35, local copies, waits for them, and re-layouts  17.9 us
    dot_general x2, matrix products, exchange_term(): jnp.dot(exchange_basis, weights.astype(jnp.bfloat16), preferred_element_t...  12.9 us
  transfers between devices with their start and end apart: 6, of which 2 were waited for; matrix products, arithmetic and copies ran while one was open for 27% of the time, Pallas kernels for 0%

commit v1 on v0

--- a/solution.py
+++ b/solution.py
@@ -28,7 +28,7 @@
     partial_sum = lax.dot_general(
         exchange_basis, summed, (((0,), (0,)), ((), ())), preferred_element_type=jnp.float32
     )
-    weights = lax.psum(partial_sum, ("wide", "narrow"))
+    weights = lax.psum(lax.psum(partial_sum, "wide"), "narrow")
     return jnp.dot(exchange_basis, weights.astype(jnp.bfloat16), preferred_element_type=jnp.float32)
 
 

time: 615 us -> 1010 us (1.64)
  waiting for transfers between devices: 72.3 us -> 570 us
  blocking collectives: 181 us -> 82.2 us
    psum x0 -> x2, waiting for transfers between devices: none -> 504 us  [exchange_term(): weights = lax.psum(lax.psum(partial_sum, 'wide'), 'narrow')]
    psum x2, blocking collectives: 181 us -> 82.2 us  [exchange_term(): weights = lax.psum(lax.psum(partial_sum, 'wide'), 'narrow')]
  transfers between devices with their start and end apart: 6 -> 8, of which waited for: 2 -> 4; matrix products, arithmetic and copies ran while one was open for 27% -> 16% of each run, Pallas kernels for 0% -> 0%
where the time goes in v1:
time: 1010 us
  waiting for transfers between devices  570 us (56%)
  local copies, waits for them, and re-layouts  285 us (28%)
  blocking collectives  82.2 us (8%)
  matrix products  50.1 us (5%)
  between operations  16.1 us (2%)
    psum x2, waiting for transfers between devices, exchange_term(): weights = lax.psum(lax.psum(partial_sum, 'wide'), 'narrow')  504 us
    gather x4, local copies, waits for them, and re-layouts, block_product(): tiles = source[indices]  254 us
    psum x2, blocking collectives, exchange_term(): weights = lax.psum(lax.psum(partial_sum, 'wide'), 'narrow')  82.2 us
    ppermute x2, waiting for transfers between devices, swapped(): lax.ppermute(array, axis, [(i, i ^ 1 << stride) for i in range(lax.axis_s...  66.5 us
    dot_general x4, matrix products, block_product(): jnp.einsum('bnij,bnjc->bic', kernel, tiles, preferred_element_type=jnp.fl...  32.4 us
  transfers between devices with their start and end apart: 8, of which 4 were waited for; matrix products, arithmetic and copies ran while one was open for 16% of the time, Pallas kernels for 0%

profile of v1, /device:TPU:1, one launch (start us, length us, event | category | flops | bytes accessed | tf_op | source)
XLA Modules:
  0.0 1010.6 jit_solution(12026246613577305970)
XLA Ops:
  8.0 0.0 all-reduce.5.cloned.1.call-start
  8.1 4.5 convolution_bitcast_fusion.3
  12.6 0.0 all-gather.5.cloned.1.call-start
  12.7 1.3 convert_element_type.24
  14.0 0.1 convert_element_type.25
  14.0 1.1 pad_maximum_fusion
  15.1 0.0 all-gather.5.cloned.1.call-update
  15.1 0.0 all-gather.7.cloned.1.call-start
  15.2 2.2 collective-permute-start
  17.4 32.0 %collective-permute-done = bf16[2048,256]{1,0:T(8,128)(2,1)S(1)} collective-permute-done((bf16[2048,256]{1,0:T(8,128)(2,1)}, bf16[2048,256]{1,0:T(8,128)(2,1)S(1)}, u32[]{:S(2)}, u32[]{:S(2)}) %collective-permute-start) | collective-permute-done | bytes 1048608 | tf_op jit(solution)/shard_map/ppermute | solution.py:11
  49.3 1.0 copy-done.3
  50.3 0.0 all-gather.7.cloned.1.call-update
  50.4 0.0 all-reduce.7.cloned.1.call-start
  50.4 0.3 copy.12
  50.8 1.3 copy.16
  52.1 0.5 broadcast.86
  52.6 0.7 reduce.3
  53.4 0.1 reshape.62
  53.5 0.7 gather_fusion.1
  54.2 0.1 fusion.2
  54.4 250.8 %all-reduce.5.cloned.1.call-done = f32[1024,128]{0,1:T(8,128)} async-done(((f32[1024,128]{0,1:T(8,128)}), f32[1024,128]{0,1:T(8,128)}) %all-reduce.5.cloned.1.call-update) | async-done | bytes 524304 | tf_op jit(solution)/shard_map/psum | solution.py:31
  305.2 41.1 %all-reduce.8 = bf16[1024,128]{0,1:T(8,128)(2,1)S(1)} all-reduce(f32[1024,128]{0,1:T(8,128)} %all-reduce.5.cloned.1.call-done), channel_id=1, replica_groups=mesh['wide'=32,'narrow'=4] {'narrow'}, use_global_device_ids=true, to_apply=%region_1.0 | all-reduce | flops 131072 | bytes 786432 | tf_op jit(solution)/shard_map/psum | solution.py:31
  346.3 0.0 all-gather.5.cloned.1.call-done
  346.3 63.5 %gather_fusion = bf16[16384,256]{1,0:T(8,128)(2,1)} fusion(bf16[8192,256]{1,0:T(8,128)(2,1)} %all-gather.5.cloned.1.call-done, s32[16384]{0:T(1024)S(1)} %broadcast_clamp_fusion.1), kind=kCustom, calls=%fused_computation | custom fusion | bytes 16842752 | tf_op jit(solution)/shard_map/gather | solution.py:16
  409.8 8.1 fusion.10
  417.9 0.1 fusion.8
  418.1 1.4 copy.32
  419.5 1.3 copy.34
  420.8 63.5 %gather_fusion.2 = bf16[16384,256]{1,0:T(8,128)(2,1)} fusion(bf16[8192,256]{1,0:T(8,128)(2,1)} %all-gather.7.cloned.1.call-done, s32[16384]{0:T(1024)S(1)} %broadcast_clamp_fusion), kind=kCustom, calls=%fused_computation.2 | custom fusion | bytes 16842752 | tf_op jit(solution)/shard_map/gather | solution.py:16
  484.3 8.1 fusion.11
  492.4 0.1 fusion.9
  492.6 1.3 copy.33
  493.9 0.3 copy.35
  494.3 5.5 fusion.5
  499.8 1.0 copy-done.5
  500.7 0.4 copy-done.6
  501.1 1.5 convolution_bitcast_fusion.2
  502.6 0.0 all-reduce.7.cloned.1.call-update
  502.6 0.0 all-gather.9.cloned.1.call-start
  502.7 1.0 pad_maximum_fusion.1
  503.7 0.0 all-gather.9.cloned.1.call-update
  503.7 0.0 all-gather.11.cloned.1.call-start
  503.8 0.3 collective-permute-start.1
  504.1 34.5 %collective-permute-done.1 = bf16[2048,256]{0,1:T(8,128)(2,1)S(1)} collective-permute-done((bf16[2048,256]{0,1:T(8,128)(2,1)}, bf16[2048,256]{0,1:T(8,128)(2,1)S(1)}, u32[]{:S(2)}, u32[]{:S(2)}) %collective-permute-start.1) | collective-permute-done | bytes 1048608 | tf_op jit(solution)/shard_map/ppermute | solution.py:11
  538.6 1.0 copy-done.4
  539.5 0.0 all-gather.11.cloned.1.call-update
  539.5 252.7 %all-reduce.7.cloned.1.call-done = f32[1024,128]{0,1:T(8,128)} async-done(((f32[1024,128]{0,1:T(8,128)}), f32[1024,128]{0,1:T(8,128)}) %all-reduce.7.cloned.1.call-update) | async-done | bytes 524304 | tf_op jit(solution)/shard_map/psum | solution.py:31
  792.2 41.1 %all-reduce.9 = bf16[1024,128]{0,1:T(8,128)(2,1)S(1)} all-reduce(f32[1024,128]{0,1:T(8,128)} %all-reduce.7.cloned.1.call-done), channel_id=1, replica_groups=mesh['wide'=32,'narrow'=4] {'narrow'}, use_global_device_ids=true, to_apply=%region_3.0 | all-reduce | flops 131072 | bytes 786432 | tf_op jit(solution)/shard_map/psum | solution.py:31
  833.3 0.0 all-gather.9.cloned.1.call-done
  833.4 6.4 copy.20
  839.7 63.5 %gather_fusion.3 = bf16[16384,256]{1,0:T(8,128)(2,1)} fusion(bf16[8192,256]{1,0:T(8,128)(2,1)} %copy.20, s32[16384]{0:T(1024)S(1)} %broadcast_clamp_fusion.1), kind=kCustom, calls=%fused_computation.3 | custom fusion | bytes 16842752 | tf_op jit(solution)/shard_map/gather | solution.py:16
  903.3 8.1 fusion.12
  911.4 0.1 fusion.6
  911.5 0.3 copy.36
  911.8 1.3 copy.38
  913.1 6.4 copy.22
  919.5 63.5 %gather_fusion.4 = bf16[16384,256]{1,0:T(8,128)(2,1)} fusion(bf16[8192,256]{1,0:T(8,128)(2,1)} %copy.22, s32[16384]{0:T(1024)S(1)} %broadcast_clamp_fusion), kind=kCustom, calls=%fused_computation.4 | custom fusion | bytes 16842752 | tf_op jit(solution)/shard_map/gather | solution.py:16
  983.0 8.1 fusion.13
  991.1 0.1 fusion.7
  991.3 1.3 copy.37
  992.6 0.3 copy.39
  993.0 6.2 add_divide_fusion
  999.2 2.5 copy.24
  1001.7 1.3 copy.25
  (32 shorter events, 0.2 us)
Async XLA Ops:
  8.0 42.4 %copy-start.1 = (f32[2048,128]{1,0:T(8,128)S(1)}, f32[2048,128]{1,0:T(8,128)}, u32[]{:S(2)}) copy-start(f32[2048,128]{1,0:T(8,128)} %param.10) | copy-start | bytes 3145732
  8.0 5.9 copy-start.2
  8.0 44.6 %copy-start.7 = (s32[1,8192]{1,0:T(1,128)S(1)}, s32[1,8192]{1,0:T(1,128)}, u32[]{:S(2)}) copy-start(s32[1,8192]{1,0:T(1,128)} %param.18) | copy-start | bytes 98308
  8.0 45.3 %copy-start.8 = (s32[8,8]{1,0:T(8,128)S(1)}, s32[8,8]{1,0:T(8,128)}, u32[]{:S(2)}) copy-start(s32[8,8]{1,0:T(8,128)} %param.17) | copy-start | bytes 772
  8.0 46.1 %copy-start.9 = (s32[8,8]{1,0:T(8,128)S(1)}, s32[8,8]{1,0:T(8,128)}, u32[]{:S(2)}) copy-start(s32[8,8]{1,0:T(8,128)} %param.15) | copy-start | bytes 772
  8.0 297.1 %all-reduce.5.cloned.1.call-start = ((), (), s32[]{:S(2)}) async-start(), calls=%async_computation.2 | async-start | bytes 1048576 | tf_op jit(solution)/shard_map/psum | solution.py:31
  12.6 333.7 %all-gather.5.cloned.1.call-start = ((), (), s32[]{:S(2)}) async-start(), calls=%async_computation | async-start | bytes 5242880 | tf_op jit(solution)/shard_map/all_gather | solution.py:49
  15.1 405.6 %all-gather.7.cloned.1.call-start = ((), (), s32[]{:S(2)}) async-start(), calls=%async_computation.1 | async-start | bytes 5242880 | tf_op jit(solution)/shard_map/all_gather | solution.py:24
  15.2 34.2 %collective-permute-start = (bf16[2048,256]{1,0:T(8,128)(2,1)}, bf16[2048,256]{1,0:T(8,128)(2,1)S(1)}, u32[]{:S(2)}, u32[]{:S(2)}) collective-permute-start(bf16[2048,256]{1,0:T(8,128)(2,1)} %pad_maximum_fusion), channel_id=1, source_target_pairs={{0,64},{4,68},{8,72},{12,76},{16,80},{20,84},{24,88},{28,92},{32,9... | collective-permute-start | bytes 3145736 | tf_op jit(solution)/shard_map/ppermute | solution.py:11
  49.3 1.0 copy-start.3
  50.4 741.9 %all-reduce.7.cloned.1.call-start = ((), (), s32[]{:S(2)}) async-start(), calls=%async_computation.5 | async-start | bytes 1048576 | tf_op jit(solution)/shard_map/psum | solution.py:31
  492.4 1.8 copy-start.10
  492.4 1.8 copy-start.11
  494.3 6.8 copy-start
  499.7 1.0 copy-start.5
  499.7 1.3 copy-start.6
  502.6 330.7 %all-gather.9.cloned.1.call-start = ((), (), s32[]{:S(2)}) async-start(), calls=%async_computation.3 | async-start | bytes 5242880 | tf_op jit(solution)/shard_map/all_gather | solution.py:49
  503.7 409.4 %all-gather.11.cloned.1.call-start = ((), (), s32[]{:S(2)}) async-start(), calls=%async_computation.4 | async-start | bytes 5242880 | tf_op jit(solution)/shard_map/all_gather | solution.py:24
  503.8 34.8 %collective-permute-start.1 = (bf16[2048,256]{0,1:T(8,128)(2,1)}, bf16[2048,256]{0,1:T(8,128)(2,1)S(1)}, u32[]{:S(2)}, u32[]{:S(2)}) collective-permute-start(bf16[2048,256]{0,1:T(8,128)(2,1)} %pad_maximum_fusion.1), channel_id=1, source_target_pairs={{0,64},{4,68},{8,72},{12,76},{16,80},{20,84},{24,88},{28,92},{32,9... | collective-permute-start | bytes 3145736 | tf_op jit(solution)/shard_map/ppermute | solution.py:11
  538.5 1.0 copy-start.4
Sparse Core Ops, SparseCore 0:
  12.7 292.3 all-reduce.4
  502.7 289.4 all-reduce.6
Sparse Core Ops, SparseCore 1:
  15.3 52.7 all-gather.4
  69.6 38.2 all-gather.6
  505.3 47.4 all-gather.8
  554.5 39.4 all-gather.10
